TPU v7x, 512 devices: a whole 4x8x8 slice. The times are simulated.
512 devices in a mesh: row: 64 (over z, y), bundle: 8 (over x, core).
Axes of the slice: x: 4, y: 8, z: 8, core: 2. Of those that a mesh axis runs over, the one named last changes fastest.
Arguments:
- vectors: float32 [256, 131072], P('bundle', 'row'), may hold values from -6 to 6
- blocks: float32 [2048, 64, 384], P('row'), may hold values from -0.30618622 to 0.30618622, as said below
- columns: int32 [2048, 6], P('row'), may hold values from 0 to 2047, as said below
- bounds: float32 [2], replicated, may hold values from -0.9 to 0.5, as said below
Outputs:
- basis: float32 [256, 131072], P(None, ('row', 'bundle'))
- factor: float32 [256, 256], replicated
Inputs may be any that keep to these rules, and one draw needn't show every extreme that they name: Slot 0 of block row i is i itself; every block column of block row i lies within 32 block rows of i, counted cyclically over the 2048 block rows, and a distance of exactly 32 occurs; columns of one block row may repeat. `blocks`: together with columns they make H symmetric. bounds[0] < 0 < bounds[1].
All inputs are finite; a program needn't handle non-finite values.
Results may differ from a plain program's by a relative error of at most 0.00011.
Values sent between devices are 32-bit elements; how exact they have to be, the bound alone decides.
No kernel may reach another device: no remote copies, remote signals or barrier semaphores. Data moves between devices by JAX's collectives and lax.ppermute only.
A program may use at most 64 MiB of HBM per device.

v0:
```python
import jax
import jax.numpy as jnp
from jax import lax
from jax.sharding import PartitionSpec as P


def extended_2(block, sides, width):
    for axis, dim in sides:
        count = lax.axis_size(axis)
        forward = [(i, i + 1) for i in range(count - 1)]
        forward.append((count - 1, 0))
        backward = [(target, source) for source, target in forward]
        low = lax.ppermute(
            lax.slice_in_dim(block, block.shape[dim] - width, None, axis=dim), axis, forward
        )
        high = lax.ppermute(lax.slice_in_dim(block, 0, width, axis=dim), axis, backward)
        block = jnp.concatenate([low, block, high], axis=dim)
    return block


def local(vectors, blocks, columns, bounds):
    block_rows = blocks.shape[0]
    block_size = blocks.shape[1]
    slot_count = columns.shape[1]
    row_count = lax.axis_size("row")
    total_rows = block_rows * row_count
    first_row = lax.axis_index("row") * block_rows
    center = (bounds[0] + bounds[1]) * 0.5
    half = (bounds[1] - bounds[0]) * 0.5
    local_cols = jnp.mod(columns - first_row + block_rows, total_rows).reshape(-1)

    def apply_operator(field):
        extended = extended_2(field, (("row", 1),), block_rows * block_size)
        width = field.shape[0]
        extended3 = extended.reshape(width, 3 * block_rows, block_size)
        picked = jnp.take(extended3, local_cols, axis=1).reshape(
            width, block_rows, slot_count * block_size
        )
        result = jnp.einsum("iam,cim->cia", blocks, picked, precision=lax.Precision.HIGHEST)
        return result.reshape(width, block_rows * block_size)

    first = (apply_operator(vectors) - center * vectors) / half
    second = 2.0 * (apply_operator(first) - center * first) / half - vectors
    filtered = 2.0 * (apply_operator(second) - center * second) / half - first
    stacked = lax.all_to_all(filtered, "bundle", split_axis=1, concat_axis=0, tiled=True)
    gram = jnp.dot(
        stacked, stacked.T, precision=lax.Precision.HIGHEST, preferred_element_type=jnp.float32
    )
    gram = lax.psum(gram, ("row", "bundle"))
    lower = jnp.linalg.cholesky(gram)
    basis = jax.scipy.linalg.solve_triangular(lower, stacked, lower=True)
    return (basis, lower.T)


def solution(mesh):
    placed = (P("bundle", "row"), P("row", None, None), P("row", None), P())
    return jax.shard_map(
        local,
        mesh=mesh,
        in_specs=placed,
        out_specs=(P(None, ("row", "bundle")), P()),
        check_vma=False,
    )
```

profile of v0, /device:TPU:23, one launch (start us, length us, event | category | flops | bytes accessed | tf_op | source)
XLA Modules:
  0.0 516.4 jit_solution(1491135728791172816)
XLA Ops:
  7.2 3.5 collective-permute-start
  17.6 3.5 collective-permute-done.1
  23.1 2.9 reshape.69
  26.0 3.5 copy.10
  29.5 3.8 gather_fusion
  35.4 3.5 copy.11
  38.9 3.8 reshape.71
  42.7 5.6 %fusion.6 = f32[32,32,64]{2,0,1:T(8,128)S(1)} fusion(f32[32,64,384]{2,1,0:T(8,128)S(1)} %copy-done, f32[32,32,384]{2,1,0:T(8,128)} %reshape.71), kind=kOutput, calls=%fused_computation.14 | convolution fusion | flops 301989888 | bytes 4980736 | tf_op jit(solution)/shard_map/iam,cim->cia/dot_general | solution.py:39
  52.4 4.3 collective-permute-start.2
  60.6 3.7 collective-permute-done.3
  65.3 2.9 reshape.73
  68.2 3.5 copy.14
  71.7 3.8 gather_fusion.1
  77.7 3.5 copy.15
  81.1 3.8 reshape.74
  84.9 5.6 %fusion.9 = f32[32,32,64]{2,0,1:T(8,128)S(1)} fusion(f32[32,64,384]{2,1,0:T(8,128)S(1)} %copy-done, f32[32,32,384]{2,1,0:T(8,128)} %reshape.74), kind=kOutput, calls=%fused_computation.15 | convolution fusion | flops 301989888 | bytes 4980736 | tf_op jit(solution)/shard_map/iam,cim->cia/dot_general | solution.py:39
  94.6 3.4 collective-permute-start.4
  98.1 4.0 collective-permute-start.5
  106.4 2.9 reshape.76
  109.3 3.5 copy.18
  112.8 3.8 gather_fusion.2
  118.8 3.5 copy.19
  122.2 3.8 reshape.77
  126.0 5.6 %fusion.12 = f32[32,32,64]{2,0,1:T(8,128)S(1)} fusion(f32[32,64,384]{2,1,0:T(8,128)S(1)} %copy-done, f32[32,32,384]{2,1,0:T(8,128)} %reshape.77), kind=kOutput, calls=%fused_computation.16 | convolution fusion | flops 301989888 | bytes 4980736 | tf_op jit(solution)/shard_map/iam,cim->cia/dot_general | solution.py:39
  136.5 8.2 %all-to-all-start = ((f32[32,8,256]{2,0,1:T(8,128)}), f32[32,8,256]{2,0,1:T(8,128)S(1)}, u32[]{:S(2)}, u32[]{:S(2)}) async-start(f32[32,8,256]{2,0,1:T(8,128)} %bitcast.65), calls=%async_computation | async-start | bytes 524288 | tf_op jit(solution)/shard_map/all_to_all | solution.py:45
  144.9 4.6 all-to-all-done
  151.3 277.9 %all-reduce.3.cloned.1.call-done = f32[256,256]{0,1:T(8,128)} async-done(((f32[256,256]{0,1:T(8,128)}), f32[256,256]{0,1:T(8,128)}) %all-reduce.3.cloned.1.call-update) | async-done | bytes 262160 | tf_op jit(solution)/shard_map/psum | solution.py:49
  431.9 11.7 %cholesky.50 = f32[128,128]{1,0:T(8,128)S(1)} custom-call(f32[128,128]{1,0:T(8,128)S(1)} %cholesky.118), custom_call_target="Cholesky" | custom-call | tf_op jit(solution)/shard_map/jit(cholesky)/cholesky | solution.py:50
  445.8 11.3 %custom-call.15 = f32[1,128,128]{1,2,0:T(8,128)} custom-call(f32[1,128,128]{2,1,0:T(8,128)} %get-tuple-element.32), custom_call_target="InvertDiagBlocksLowerTriangular" | custom-call | tf_op jit(solution)/shard_map/jit(cholesky)/cholesky | solution.py:50
  459.8 13.2 %cholesky.105 = f32[128,128]{1,0:T(8,128)} custom-call(f32[128,128]{1,0:T(8,128)} %convolution_subtract_fusion.1), custom_call_target="Cholesky" | custom-call | tf_op jit(solution)/shard_map/jit(cholesky)/cholesky | solution.py:50
  477.7 5.3 %while.1 = (s32[]{:T(128)}, f32[256,256]{1,0:T(8,128)S(1)}, s32[2,2]{1,0:T(2,128)S(1)}, f32[2,128,128]{2,1,0:T(8,128)}, s32[]{:T(128)}) while((s32[]{:T(128)}, f32[256,256]{1,0:T(8,128)S(1)}, s32[2,2]{1,0:T(2,128)S(1)}, f32[2,128,128]{2,1,0:T(8,128)}, s32[]{:T(128)}) %tuple.33), condition=%wide.while_cond, body=%wide.while_body.sunk | while | flops 2 | bytes 132705 | solution.py:51
  482.9 21.1 %custom-call.16 = f32[2,128,128]{1,2,0:T(8,128)} custom-call(f32[2,128,128]{2,1,0:T(8,128)} %get-tuple-element.10), custom_call_target="InvertDiagBlocksLowerTriangular" | custom-call | tf_op jit(solution)/shard_map/jit(_solve_triangular)/triangular_solve | solution.py:51
  (67 shorter events, 58.3 us)
Async XLA Ops:
  7.2 35.5 %copy-start = (f32[32,64,384]{2,1,0:T(8,128)S(1)}, f32[32,64,384]{2,1,0:T(8,128)}, u32[]{:S(2)}) copy-start(f32[32,64,384]{2,1,0:T(8,128)} %param.7) | copy-start | bytes 9437188
  7.2 10.4 %collective-permute-start = (f32[32,2048]{1,0:T(8,128)}, f32[32,2048]{1,0:T(8,128)S(1)}, u32[]{:S(2)}, u32[]{:S(2)}) collective-permute-start(f32[32,2048]{1,0:T(8,128)} %param.6), channel_id=1, source_target_pairs={{0,8},{8,16},{16,24},{24,32},{32,40},{40,48},{48,56},{56,64},{64,7... | collective-permute-start | bytes 786440 | tf_op jit(solution)/shard_map/ppermute | solution.py:13
  10.7 10.5 %collective-permute-start.1 = (f32[32,2048]{1,0:T(8,128)}, f32[32,2048]{1,0:T(8,128)}, u32[]{:S(2)}, u32[]{:S(2)}) collective-permute-start(f32[32,2048]{1,0:T(8,128)} %param.6), channel_id=1, source_target_pairs={{8,0},{16,8},{24,16},{32,24},{40,32},{48,40},{56,48},{64,56},{72,6... | collective-permute-start | bytes 786440 | tf_op jit(solution)/shard_map/ppermute | solution.py:16
  52.4 8.2 %collective-permute-start.2 = (f32[32,2048]{1,0:T(8,128)S(1)}, f32[32,2048]{1,0:T(8,128)S(1)}, u32[]{:S(2)}, u32[]{:S(2)}) collective-permute-start(f32[32,2048]{1,0:T(8,128)S(1)} %subtract_divide_fusion), channel_id=1, source_target_pairs={{0,8},{8,16},{16,24},{24,32},{32,40},{40,48},{48,56},{56,64},{64,7... | collective-permute-start | bytes 786440 | tf_op jit(solution)/shard_map/ppermute | solution.py:13
  56.7 7.7 %collective-permute-start.3 = (f32[32,2048]{1,0:T(8,128)S(1)}, f32[32,2048]{1,0:T(8,128)S(1)}, u32[]{:S(2)}, u32[]{:S(2)}) collective-permute-start(f32[32,2048]{1,0:T(8,128)S(1)} %subtract_divide_fusion), channel_id=1, source_target_pairs={{8,0},{16,8},{24,16},{32,24},{40,32},{48,40},{56,48},{64,56},{72,6... | collective-permute-start | bytes 786440 | tf_op jit(solution)/shard_map/ppermute | solution.py:16
  94.6 10.8 %copy-start.1 = (f32[32,2048]{1,0:T(8,128)}, f32[32,2048]{1,0:T(8,128)S(1)}, u32[]{:S(2)}) copy-start(f32[32,2048]{1,0:T(8,128)S(1)} %divide_subtract_fusion.1) | copy-start | bytes 786436
  94.6 9.7 %collective-permute-start.4 = (f32[32,2048]{1,0:T(8,128)S(1)}, f32[32,2048]{1,0:T(8,128)S(1)}, u32[]{:S(2)}, u32[]{:S(2)}) collective-permute-start(f32[32,2048]{1,0:T(8,128)S(1)} %divide_subtract_fusion.1), channel_id=1, source_target_pairs={{0,8},{8,16},{16,24},{24,32},{32,40},{40,48},{48,56},{56,64},{64,7... | collective-permute-start | bytes 786440 | tf_op jit(solution)/shard_map/ppermute | solution.py:13
  98.1 7.4 %collective-permute-start.5 = (f32[32,2048]{1,0:T(8,128)S(1)}, f32[32,2048]{1,0:T(8,128)S(1)}, u32[]{:S(2)}, u32[]{:S(2)}) collective-permute-start(f32[32,2048]{1,0:T(8,128)S(1)} %divide_subtract_fusion.1), channel_id=1, source_target_pairs={{8,0},{16,8},{24,16},{32,24},{40,32},{48,40},{56,48},{64,56},{72,6... | collective-permute-start | bytes 786440 | tf_op jit(solution)/shard_map/ppermute | solution.py:16
  136.5 13.0 %all-to-all-start = ((f32[32,8,256]{2,0,1:T(8,128)}), f32[32,8,256]{2,0,1:T(8,128)S(1)}, u32[]{:S(2)}, u32[]{:S(2)}) async-start(f32[32,8,256]{2,0,1:T(8,128)} %bitcast.65), calls=%async_computation | async-start | bytes 524288 | tf_op jit(solution)/shard_map/all_to_all | solution.py:45
  144.7 284.5 %all-reduce.3.cloned.1.call-start = ((), (), s32[]{:S(2)}) async-start(), calls=%async_computation.1 | async-start | bytes 524288 | tf_op jit(solution)/shard_map/psum | solution.py:49
  431.2 0.7 copy-start.3
  443.6 0.6 copy-start.4
  473.9 2.0 copy-start.2
Sparse Core Ops, SparseCore 0:
  151.0 278.0 all-reduce.2
where the time goes:
time: 525 us; the launch traced here: 516 us
  waiting for transfers between devices  295 us (56%)
  other arithmetic  77.2 us (15%)
  local copies, waits for them, and re-layouts  74.4 us (14%)
  starting transfers between devices  28.1 us (5%)
  matrix products  23.4 us (4%)
  between operations  18.4 us (4%)
    psum x1, waiting for transfers between devices, local(): gram = lax.psum(gram, ('row', 'bundle'))  278 us
    another operation x6, other arithmetic, local(): lower = jnp.linalg.cholesky(gram)  38.4 us
    another operation x3, other arithmetic, local(): basis = jax.scipy.linalg.solve_triangular(lower, stacked, lower=True)  21.8 us
    reshape x6, local copies, waits for them, and re-layouts, apply_operator(): extended3 = extended.reshape(width, 3 * block_rows, block_size)  19.2 us
    dot_general x3, matrix products, apply_operator(): jnp.einsum('iam,cim->cia', blocks, picked, precision=lax.Precision.HIGHEST)  16.8 us
    gather x3, local copies, waits for them, and re-layouts, apply_operator(): jnp.take(extended3, local_cols, axis=1)  11.4 us
    reshape x3, local copies, waits for them, and re-layouts, apply_operator(): jnp.take(extended3, local_cols, axis=1)  11.3 us
    ppermute x3, starting transfers between devices, extended_2(): lax.ppermute(lax.slice_in_dim(block, block.shape[dim] - width, None, axis...  11.2 us
  transfers between devices with their start and end apart: 8, of which 7 were waited for; matrix products, arithmetic and copies ran while one was open for 1% of the time, Pallas kernels for 0%

commit v1 on v0

--- a/solution.py
+++ b/solution.py
@@ -46,7 +46,7 @@
     gram = jnp.dot(
         stacked, stacked.T, precision=lax.Precision.HIGHEST, preferred_element_type=jnp.float32
     )
-    gram = lax.psum(gram, ("row", "bundle"))
+    gram = lax.psum(lax.psum(gram, "row"), "bundle")
     lower = jnp.linalg.cholesky(gram)
     basis = jax.scipy.linalg.solve_triangular(lower, stacked, lower=True)
     return (basis, lower.T)

time: 525 us -> 476 us (0.907)
  the two profiles are of different devices: /device:TPU:23 before, /device:TPU:8 now
where the time goes in v1:
time: 476 us; the launch traced here: 467 us
  waiting for transfers between devices  230 us (48%)
  other arithmetic  77.2 us (16%)
  local copies, waits for them, and re-layouts  74 us (16%)
  starting transfers between devices  31.9 us (7%)
  matrix products  23.4 us (5%)
  between operations  18.5 us (4%)
  blocking collectives  11.6 us (2%)
    psum x2, waiting for transfers between devices, local(): gram = lax.psum(lax.psum(gram, 'row'), 'bundle')  222 us
    another operation x6, other arithmetic, local(): lower = jnp.linalg.cholesky(gram)  38.4 us
    ppermute x3, starting transfers between devices, extended_2(): lax.ppermute(lax.slice_in_dim(block, 0, width, axis=dim), axis, backward)  22.5 us
    another operation x3, other arithmetic, local(): basis = jax.scipy.linalg.solve_triangular(lower, stacked, lower=True)  21.8 us
    reshape x6, local copies, waits for them, and re-layouts, apply_operator(): extended3 = extended.reshape(width, 3 * block_rows, block_size)  19.2 us
    dot_general x3, matrix products, apply_operator(): jnp.einsum('iam,cim->cia', blocks, picked, precision=lax.Precision.HIGHEST)  16.8 us
    all_to_all x1, blocking collectives, local(): lax.all_to_all(filtered, 'bundle', split_axis=1, concat_axis=0, tiled=True)  11.6 us
    gather x3, local copies, waits for them, and re-layouts, apply_operator(): jnp.take(extended3, local_cols, axis=1)  11.4 us
  transfers between devices with their start and end apart: 8, of which 6 were waited for; matrix products, arithmetic and copies ran while one was open for 1% of the time, Pallas kernels for 0%

profile of v1, /device:TPU:8, one launch (start us, length us, event | category | flops | bytes accessed | tf_op | source)
XLA Modules:
  0.0 467.1 jit_solution(12348188963206577727)
XLA Ops:
  7.2 3.8 collective-permute-start
  11.0 6.1 %collective-permute-start.1 = (f32[32,2048]{1,0:T(8,128)}, f32[32,2048]{1,0:T(8,128)}, u32[]{:S(2)}, u32[]{:S(2)}) collective-permute-start(f32[32,2048]{1,0:T(8,128)} %param.6), channel_id=1, source_target_pairs={{8,0},{16,8},{24,16},{32,24},{40,32},{48,40},{56,48},{64,56},{72,6... | collective-permute-start | bytes 786440 | tf_op jit(solution)/shard_map/ppermute | solution.py:16
  24.0 2.9 reshape.69
  26.9 3.5 copy.10
  30.4 3.8 gather_fusion
  36.4 3.5 copy.11
  39.8 3.8 reshape.71
  43.6 5.6 %fusion.6 = f32[32,32,64]{2,0,1:T(8,128)S(1)} fusion(f32[32,64,384]{2,1,0:T(8,128)S(1)} %copy-done, f32[32,32,384]{2,1,0:T(8,128)} %reshape.71), kind=kOutput, calls=%fused_computation.14 | convolution fusion | flops 301989888 | bytes 4980736 | tf_op jit(solution)/shard_map/iam,cim->cia/dot_general | solution.py:39
  53.3 3.5 collective-permute-start.2
  56.8 8.4 %collective-permute-start.3 = (f32[32,2048]{1,0:T(8,128)S(1)}, f32[32,2048]{1,0:T(8,128)S(1)}, u32[]{:S(2)}, u32[]{:S(2)}) collective-permute-start(f32[32,2048]{1,0:T(8,128)S(1)} %subtract_divide_fusion), channel_id=1, source_target_pairs={{8,0},{16,8},{24,16},{32,24},{40,32},{48,40},{56,48},{64,56},{72,6... | collective-permute-start | bytes 786440 | tf_op jit(solution)/shard_map/ppermute | solution.py:16
  65.3 3.0 collective-permute-done.2
  70.4 2.9 reshape.73
  73.3 3.5 copy.14
  76.8 3.8 gather_fusion.1
  82.8 3.5 copy.15
  86.3 3.8 reshape.74
  90.0 5.6 %fusion.9 = f32[32,32,64]{2,0,1:T(8,128)S(1)} fusion(f32[32,64,384]{2,1,0:T(8,128)S(1)} %copy-done, f32[32,32,384]{2,1,0:T(8,128)} %reshape.74), kind=kOutput, calls=%fused_computation.15 | convolution fusion | flops 301989888 | bytes 4980736 | tf_op jit(solution)/shard_map/iam,cim->cia/dot_general | solution.py:39
  101.7 7.9 %collective-permute-start.5 = (f32[32,2048]{1,0:T(8,128)S(1)}, f32[32,2048]{1,0:T(8,128)S(1)}, u32[]{:S(2)}, u32[]{:S(2)}) collective-permute-start(f32[32,2048]{1,0:T(8,128)S(1)} %divide_subtract_fusion.1), channel_id=1, source_target_pairs={{8,0},{16,8},{24,16},{32,24},{40,32},{48,40},{56,48},{64,56},{72,6... | collective-permute-start | bytes 786440 | tf_op jit(solution)/shard_map/ppermute | solution.py:16
  114.2 2.9 reshape.76
  117.2 3.5 copy.18
  120.6 3.8 gather_fusion.2
  126.6 3.5 copy.19
  130.1 3.8 reshape.77
  133.9 5.6 %fusion.12 = f32[32,32,64]{2,0,1:T(8,128)S(1)} fusion(f32[32,64,384]{2,1,0:T(8,128)S(1)} %copy-done, f32[32,32,384]{2,1,0:T(8,128)} %reshape.77), kind=kOutput, calls=%fused_computation.16 | convolution fusion | flops 301989888 | bytes 4980736 | tf_op jit(solution)/shard_map/iam,cim->cia/dot_general | solution.py:39
  143.7 11.6 %all_to_all.19 = f32[32,8,256]{2,0,1:T(8,128)S(1)} all-to-all(f32[32,8,256]{2,0,1:T(8,128)S(1)} %bitcast.65), channel_id=1, replica_groups=mesh['row'=64,'bundle'=8] {'bundle'}, dimensions={1} | all-to-all | bytes 524288 | tf_op jit(solution)/shard_map/all_to_all | solution.py:45
  156.7 152.8 %all-reduce.4.cloned.1.call-done = f32[256,256]{0,1:T(8,128)} async-done(((f32[256,256]{0,1:T(8,128)}), f32[256,256]{0,1:T(8,128)}) %all-reduce.4.cloned.1.call-update) | async-done | bytes 262160 | tf_op jit(solution)/shard_map/psum | solution.py:49
  310.2 69.5 %all-reduce.6.cloned.1.call-done = f32[256,256]{0,1:T(8,128)} async-done(((f32[256,256]{0,1:T(8,128)}), f32[256,256]{0,1:T(8,128)}) %all-reduce.6.cloned.1.call-update) | async-done | bytes 262160 | tf_op jit(solution)/shard_map/psum | solution.py:49
  382.5 11.7 %cholesky.50 = f32[128,128]{1,0:T(8,128)S(1)} custom-call(f32[128,128]{1,0:T(8,128)S(1)} %cholesky.118), custom_call_target="Cholesky" | custom-call | tf_op jit(solution)/shard_map/jit(cholesky)/cholesky | solution.py:50
  396.3 11.3 %custom-call.15 = f32[1,128,128]{1,2,0:T(8,128)} custom-call(f32[1,128,128]{2,1,0:T(8,128)} %get-tuple-element.32), custom_call_target="InvertDiagBlocksLowerTriangular" | custom-call | tf_op jit(solution)/shard_map/jit(cholesky)/cholesky | solution.py:50
  410.4 13.2 %cholesky.105 = f32[128,128]{1,0:T(8,128)} custom-call(f32[128,128]{1,0:T(8,128)} %convolution_subtract_fusion.1), custom_call_target="Cholesky" | custom-call | tf_op jit(solution)/shard_map/jit(cholesky)/cholesky | solution.py:50
  428.3 5.4 %while.1 = (s32[]{:T(128)}, f32[256,256]{1,0:T(8,128)S(1)}, s32[2,2]{1,0:T(2,128)S(1)}, f32[2,128,128]{2,1,0:T(8,128)}, s32[]{:T(128)}) while((s32[]{:T(128)}, f32[256,256]{1,0:T(8,128)S(1)}, s32[2,2]{1,0:T(2,128)S(1)}, f32[2,128,128]{2,1,0:T(8,128)}, s32[]{:T(128)}) %tuple.33), condition=%wide.while_cond, body=%wide.while_body.sunk | while | flops 2 | bytes 132705 | solution.py:51
  433.7 21.1 %custom-call.16 = f32[2,128,128]{1,2,0:T(8,128)} custom-call(f32[2,128,128]{2,1,0:T(8,128)} %get-tuple-element.10), custom_call_target="InvertDiagBlocksLowerTriangular" | custom-call | tf_op jit(solution)/shard_map/jit(_solve_triangular)/triangular_solve | solution.py:51
  (69 shorter events, 55.3 us)
Async XLA Ops:
  7.2 36.4 %copy-start = (f32[32,64,384]{2,1,0:T(8,128)S(1)}, f32[32,64,384]{2,1,0:T(8,128)}, u32[]{:S(2)}) copy-start(f32[32,64,384]{2,1,0:T(8,128)} %param.7) | copy-start | bytes 9437188
  7.2 302.3 %all-reduce.4.cloned.1.call-start = ((), (), s32[]{:S(2)}) async-start(), calls=%async_computation.1 | async-start | bytes 524288 | tf_op jit(solution)/shard_map/psum | solution.py:49
  7.2 14.7 %collective-permute-start = (f32[32,2048]{1,0:T(8,128)}, f32[32,2048]{1,0:T(8,128)S(1)}, u32[]{:S(2)}, u32[]{:S(2)}) collective-permute-start(f32[32,2048]{1,0:T(8,128)} %param.6), channel_id=1, source_target_pairs={{0,8},{8,16},{16,24},{24,32},{32,40},{40,48},{48,56},{56,64},{64,7... | collective-permute-start | bytes 786440 | tf_op jit(solution)/shard_map/ppermute | solution.py:13
  11.0 11.0 %collective-permute-start.1 = (f32[32,2048]{1,0:T(8,128)}, f32[32,2048]{1,0:T(8,128)}, u32[]{:S(2)}, u32[]{:S(2)}) collective-permute-start(f32[32,2048]{1,0:T(8,128)} %param.6), channel_id=1, source_target_pairs={{8,0},{16,8},{24,16},{32,24},{40,32},{48,40},{56,48},{64,56},{72,6... | collective-permute-start | bytes 786440 | tf_op jit(solution)/shard_map/ppermute | solution.py:16
  53.3 14.9 %collective-permute-start.2 = (f32[32,2048]{1,0:T(8,128)S(1)}, f32[32,2048]{1,0:T(8,128)S(1)}, u32[]{:S(2)}, u32[]{:S(2)}) collective-permute-start(f32[32,2048]{1,0:T(8,128)S(1)} %subtract_divide_fusion), channel_id=1, source_target_pairs={{0,8},{8,16},{16,24},{24,32},{32,40},{40,48},{48,56},{56,64},{64,7... | collective-permute-start | bytes 786440 | tf_op jit(solution)/shard_map/ppermute | solution.py:13
  56.8 12.6 %collective-permute-start.3 = (f32[32,2048]{1,0:T(8,128)S(1)}, f32[32,2048]{1,0:T(8,128)S(1)}, u32[]{:S(2)}, u32[]{:S(2)}) collective-permute-start(f32[32,2048]{1,0:T(8,128)S(1)} %subtract_divide_fusion), channel_id=1, source_target_pairs={{8,0},{16,8},{24,16},{32,24},{40,32},{48,40},{56,48},{64,56},{72,6... | collective-permute-start | bytes 786440 | tf_op jit(solution)/shard_map/ppermute | solution.py:16
  99.8 13.5 %copy-start.1 = (f32[32,2048]{1,0:T(8,128)}, f32[32,2048]{1,0:T(8,128)S(1)}, u32[]{:S(2)}) copy-start(f32[32,2048]{1,0:T(8,128)S(1)} %divide_subtract_fusion.1) | copy-start | bytes 786436
  99.8 12.3 %collective-permute-start.4 = (f32[32,2048]{1,0:T(8,128)S(1)}, f32[32,2048]{1,0:T(8,128)S(1)}, u32[]{:S(2)}, u32[]{:S(2)}) collective-permute-start(f32[32,2048]{1,0:T(8,128)S(1)} %divide_subtract_fusion.1), channel_id=1, source_target_pairs={{0,8},{8,16},{16,24},{24,32},{32,40},{40,48},{48,56},{56,64},{64,7... | collective-permute-start | bytes 786440 | tf_op jit(solution)/shard_map/ppermute | solution.py:13
  101.7 11.6 %collective-permute-start.5 = (f32[32,2048]{1,0:T(8,128)S(1)}, f32[32,2048]{1,0:T(8,128)S(1)}, u32[]{:S(2)}, u32[]{:S(2)}) collective-permute-start(f32[32,2048]{1,0:T(8,128)S(1)} %divide_subtract_fusion.1), channel_id=1, source_target_pairs={{8,0},{16,8},{24,16},{32,24},{40,32},{48,40},{56,48},{64,56},{72,6... | collective-permute-start | bytes 786440 | tf_op jit(solution)/shard_map/ppermute | solution.py:16
  156.4 223.3 %all-reduce.6.cloned.1.call-start = ((), (), s32[]{:S(2)}) async-start(), calls=%async_computation.2 | async-start | bytes 524288 | tf_op jit(solution)/shard_map/psum | solution.py:49
  381.8 0.7 copy-start.3
  394.2 0.6 copy-start.4
  424.5 2.0 copy-start.2
Sparse Core Ops, SparseCore 0:
  156.5 152.8 all-reduce.3
  311.8 67.8 all-reduce.5
